TPU v7x, 256 devices: a whole 4x4x8 slice. The times are simulated.
256 devices in a mesh: slab: 16 (over z_hi, x, core), chan: 16 (over y, z_lo).
Axes of the slice: x: 4, y: 4, z: 8 (z_hi: 2, z_lo: 4; z = z_hi * 4 + z_lo), core: 2. Of those that a mesh axis runs over, the one named last changes fastest.
Arguments:
- activations: bfloat16 [2, 128, 32, 16384], P(None, 'chan', 'slab'), may hold values from -6 to 6
- out_grad: bfloat16 [2, 256, 16, 4096], P(None, 'chan', 'slab'), may hold values from -6 to 6
- weights: bfloat16 [27, 128, 256], P(None, 'chan'), may hold values from -0.109375 to 0.109375
Outputs:
- input_grad: bfloat16 [2, 128, 32, 16384], P(None, 'chan', 'slab')
- weight_grad: float32 [27, 128, 256], P(None, 'chan', 'slab')
All inputs are finite; a program needn't handle non-finite values.
Results may differ from a plain program's by a relative error of at most 0.001.
Values may be sent and summed in bfloat16 or wider, within the bound.
A program may use at most 128 MiB of HBM per device.

v0:
```python
import math

import jax
import jax.numpy as jnp
from jax import lax
from jax.sharding import PartitionSpec as P

EDGE = 128


def from_behind(x, axis, by):
    count = lax.axis_size(axis)
    pairs = [(i, i + by) for i in range(count) if 0 <= i + by < count]
    return lax.ppermute(x, axis, pairs)


def flat_back(values, amount):
    zero_part = jnp.zeros(values.shape[:-1] + (amount,), values.dtype)
    return jnp.concatenate([zero_part, values[..., : values.shape[-1] - amount]], axis=-1)


def flat_ahead(values, amount):
    zero_part = jnp.zeros(values.shape[:-1] + (amount,), values.dtype)
    return jnp.concatenate([values[..., amount:], zero_part], axis=-1)


def column_index(length, half_edge):
    return lax.iota(jnp.int32, length) % half_edge


def tap_view(volume, row_tap, col_tap, half_edge):
    cells = half_edge * half_edge
    row_phase = 0 if row_tap == 1 else 1
    col_phase = 0 if col_tap == 1 else 1
    block = row_phase * 2 + col_phase
    picked = volume[..., block * cells : (block + 1) * cells]
    if row_tap == 0:
        picked = flat_back(picked, half_edge)
    if col_tap == 0:
        picked = flat_back(picked, 1)
        keep_mask = column_index(cells, half_edge) != 0
        picked = jnp.where(keep_mask, picked, jnp.zeros_like(picked))
    return picked


def assemble(fetch, half_edge, block_cells):
    last_column = column_index(block_cells, half_edge) == half_edge - 1
    rows_even = [fetch(1, col_tap) for col_tap in range(3)]
    rows_odd = [
        fetch(2, col_tap) + flat_ahead(fetch(0, col_tap), half_edge) for col_tap in range(3)
    ]
    phases = []
    for rows in (rows_even, rows_odd):
        phases.append(rows[1])
        moved = flat_ahead(rows[0], 1)
        phases.append(rows[2] + jnp.where(last_column, jnp.zeros_like(moved), moved))
    return jnp.concatenate(phases, axis=-1)


def body(activations, out_grad, weights):
    samples, chan_local, planes, plane_cells = activations.shape
    half_edge = EDGE // 2
    cells = half_edge * half_edge
    out_planes = planes // 2
    phased = activations.reshape(samples, chan_local, out_planes, 2, plane_cells)
    even_planes = phased[:, :, :, 0]
    odd_planes = phased[:, :, :, 1]
    previous = from_behind(odd_planes[:, :, out_planes - 1], "slab", 1)
    odd_before = jnp.concatenate([previous[:, :, None], odd_planes[:, :, : out_planes - 1]], axis=2)
    depth_views = (odd_before, even_planes, odd_planes)
    following = from_behind(out_grad[:, :, 0], "slab", -1)
    source = jnp.concatenate([out_grad, following[:, :, None]], axis=2)
    signal = lax.all_gather(source, "chan", axis=1, tiled=True)
    own_planes = signal[:, :, :out_planes]
    pieces = []
    for depth_tap in range(3):
        stacked = jnp.stack(
            [
                tap_view(depth_views[depth_tap], row_tap, col_tap, half_edge)
                for row_tap in range(3)
                for col_tap in range(3)
            ]
        )
        pieces.append(
            jnp.einsum("tbcdp,bkdp->tck", stacked, own_planes, preferred_element_type=jnp.float32)
        )
    local_grad = jnp.concatenate(pieces, axis=0)
    total_cells = samples * out_planes * lax.axis_size("slab") * half_edge * half_edge
    weight_grad = lax.psum_scatter(local_grad, "slab", scatter_dimension=2, tiled=True) * (
        1.0 / math.sqrt(total_cells)
    )
    first_block = signal[:, :, 1:]
    blocks = (first_block, own_planes, own_planes)
    folded = []
    for depth_tap in range(3):
        groups = jnp.einsum(
            "tck,bkdp->tbcdp",
            weights[9 * depth_tap : 9 * depth_tap + 9],
            blocks[depth_tap],
            preferred_element_type=jnp.float32,
        )

        def fetch(row_tap, col_tap, groups=groups):
            return groups[3 * row_tap + col_tap]

        folded.append(assemble(fetch, half_edge, cells))
    shifted = folded[0]
    odd_out = folded[2] + shifted
    chan_rows = folded[1].shape[1]
    kept_cells = 4 * cells
    local_grad_in = (
        jnp.stack([folded[1], odd_out], axis=3)
        .reshape(samples, chan_rows, planes, kept_cells)
        .astype(jnp.bfloat16)
    )
    return (local_grad_in, weight_grad)


def solution(mesh):
    placed = (P(None, "chan", "slab", None), P(None, "chan", "slab", None), P(None, "chan", None))
    return jax.shard_map(
        body,
        mesh=mesh,
        in_specs=placed,
        out_specs=(P(None, "chan", "slab", None), P(None, "chan", "slab")),
        check_vma=False,
    )
```

profile of v0, /device:TPU:1, one launch (start us, length us, event | category | flops | bytes accessed | tf_op | source)
XLA Modules:
  0.0 309.1 jit_solution(10184188523158755231)
XLA Ops:
  7.2 5.2 %collective-permute-start = (bf16[2,16,4096]{2,1,0:T(8,128)(2,1)}, bf16[2,16,4096]{2,1,0:T(8,128)(2,1)S(1)}, u32[]{:S(2)}, u32[]{:S(2)}) collective-permute-start(bf16[2,16,4096]{2,1,0:T(8,128)(2,1)} %bitcast.307), channel_id=1, source_target_pairs={{16,0},{32,16},{48,32},{64,48},{80,64},{96,80},{112,96},{128,112},... | collective-permute-start | bytes 786440 | tf_op jit(solution)/shard_map/ppermute | solution.py:14
  12.4 1.8 copy.115
  14.3 1.9 collective-permute-start.1
  17.0 0.8 bitcast_dynamic-update-slice_fusion.10
  17.8 0.9 bitcast_dynamic-update-slice_fusion.8
  18.8 0.8 bitcast_dynamic-update-slice_fusion.7
  19.6 0.8 pad_maximum_fusion.1
  20.5 0.7 bitcast_dynamic-update-slice_fusion.6
  21.2 0.7 fusion.56
  21.9 0.7 fusion.55
  22.6 0.8 bitcast_dynamic-update-slice_fusion.5
  23.3 0.7 fusion.58
  24.0 0.7 fusion.54
  24.7 0.7 fusion.53
  26.2 186.9 %all-gather.2.cloned.1.call-done = bf16[2,256,2,4096]{3,1,0,2:T(8,128)(2,1)} async-done(((bf16[2,16,2,4096]{3,1,0,2:T(8,128)(2,1)}), bf16[2,256,2,4096]{3,1,0,2:T(8,128)(2,1)}) %all-gather.2.cloned.1.call-update) | async-done | bytes 8388624 | tf_op jit(solution)/shard_map/all_gather | solution.py:73
  213.1 3.1 convolution_bitcast_fusion
  216.5 1.0 fusion.72
  217.6 1.5 copy-done.6
  219.1 1.4 fusion.21
  220.5 1.4 fusion.16
  221.9 1.4 fusion.26
  223.4 1.4 copy.59
  224.8 3.0 convolution_bitcast_fusion.2
  229.2 0.6 slice.345
  231.0 3.0 convolution_bitcast_fusion.1
  235.8 1.4 pad_add_fusion.2
  237.2 3.2 %fusion.52 = (bf16[2,8,1,4096]{3,2,1,0:T(2,128)(2,1)S(1)}, bf16[2,8,1,4096]{3,2,1,0:T(2,128)(2,1)S(1)}) fusion(f32[9,2,8,1,4096]{4,0,2,1,3:T(8,128)} %copy-done, f32[2,8,1,4032]{3,2,1,0:T(1,128)S(1)} %slice.342, f32[2,8,1,4095]{3,2,1,0:T(1,128)S(1)} %pad_add_fusion.2, pred[4096]{0:T(1024)(128)(4,1)S(1)} %fusion.70, f32[2,8,1,4032]{3,2,1,0:T(1,128)S(1)} %slice.345), kind=kLoop, calls=%fused_computation.84 | loop fusion | flops 393216 | bytes 1568704 | tf_op jit(solution)/shard_map/convert.5
  240.4 1.1 pad_maximum_fusion
  242.4 2.1 copy.60
  244.4 56.3 %reduce-scatter.2.cloned.1.call-done = f32[27,8,16]{0,1,2:T(8,128)} async-done(((f32[27,8,256]{0,1,2:T(8,128)}), f32[27,8,16]{0,1,2:T(8,128)}) %reduce-scatter.2.cloned.1.call-update) | async-done | bytes 13840 | tf_op jit(solution)/shard_map/reduce_scatter | solution.py:89
  300.7 0.8 broadcast_multiply_fusion
  301.6 0.6 copy.61
  (73 shorter events, 7.0 us)
Async XLA Ops:
  7.2 206.0 %all-gather.2.cloned.1.call-start = ((), (), s32[]{:S(2)}) async-start(), calls=%async_computation.1 | async-start | bytes 8912896 | tf_op jit(solution)/shard_map/all_gather | solution.py:73
  7.2 12.3 %collective-permute-start = (bf16[2,16,4096]{2,1,0:T(8,128)(2,1)}, bf16[2,16,4096]{2,1,0:T(8,128)(2,1)S(1)}, u32[]{:S(2)}, u32[]{:S(2)}) collective-permute-start(bf16[2,16,4096]{2,1,0:T(8,128)(2,1)} %bitcast.307), channel_id=1, source_target_pairs={{16,0},{32,16},{48,32},{64,48},{80,64},{96,80},{112,96},{128,112},... | collective-permute-start | bytes 786440 | tf_op jit(solution)/shard_map/ppermute | solution.py:14
  14.3 11.2 %collective-permute-start.1 = (bf16[2,8,16384]{2,1,0:T(8,128)(2,1)S(1)}, bf16[2,8,16384]{2,1,0:T(8,128)(2,1)S(1)}, u32[]{:S(2)}, u32[]{:S(2)}) collective-permute-start(bf16[2,8,16384]{2,1,0:T(8,128)(2,1)S(1)} %get-tuple-element.32), channel_id=1, source_target_pairs={{0,16},{16,32},{32,48},{48,64},{64,80},{80,96},{96,112},{112,128},... | collective-permute-start | bytes 1572872 | tf_op jit(solution)/shard_map/ppermute | solution.py:14
  16.7 2.9 copy-start.1
  17.8 1.7 copy-start.3
  20.4 5.0 %copy-start.2 = (bf16[27,8,256]{2,1,0:T(8,128)(2,1)S(1)}, bf16[27,8,256]{2,1,0:T(8,128)(2,1)}, u32[]{:S(2)}) copy-start(bf16[27,8,256]{2,1,0:T(8,128)(2,1)} %param.5) | copy-start | bytes 331780
  20.4 280.3 %reduce-scatter.2.cloned.1.call-start = ((), (), s32[]{:S(2)}) async-start(), calls=%async_computation.2 | async-start | bytes 1114112 | tf_op jit(solution)/shard_map/reduce_scatter | solution.py:89
  213.1 6.0 %copy-start.6 = (bf16[2,256,2,4096]{3,1,0,2:T(8,128)(2,1)S(1)}, bf16[2,256,2,4096]{3,1,0,2:T(8,128)(2,1)}, u32[]{:S(2)}) copy-start(bf16[2,256,2,4096]{3,1,0,2:T(8,128)(2,1)} %all-gather.2.cloned.1.call-done) | copy-start | bytes 25165828
  216.2 4.3 %copy-start = (f32[9,2,8,1,4096]{4,0,2,1,3:T(8,128)}, f32[9,2,8,1,4096]{4,0,2,1,3:T(8,128)S(1)}, u32[]{:S(2)}) copy-start(f32[9,2,8,1,4096]{4,0,2,1,3:T(8,128)S(1)} %convolution_bitcast_fusion) | copy-start | bytes 7077892
  219.1 1.4 copy-start.5
  220.5 1.4 copy-start.4
Sparse Core Ops, SparseCore 0:
  20.5 192.5 all-gather.1
  224.9 75.7 reduce-scatter.1
where the time goes:
time: 311 us; the launch traced here: 309 us
  waiting for transfers between devices  243 us (78%)
  local copies, waits for them, and re-layouts  19.5 us (6%)
  between operations  14.5 us (5%)
  matrix products  13.3 us (4%)
  other arithmetic  11.4 us (4%)
  starting transfers between devices  7.15 us (2%)
    all_gather x1, waiting for transfers between devices, body(): signal = lax.all_gather(source, 'chan', axis=1, tiled=True)  187 us
    reduce_scatter x1, waiting for transfers between devices, body(): lax.psum_scatter(local_grad, 'slab', scatter_dimension=2, tiled=True)  56.3 us
    unnamed x35, local copies, waits for them, and re-layouts  11.8 us
    dot_general x3, matrix products, body(): jnp.einsum('tck,bkdp->tbcdp', weights[9 * depth_tap:9 * depth_tap + 9], b...  9.15 us
    ppermute x2, starting transfers between devices, from_behind(): return lax.ppermute(x, axis, pairs)  7.07 us
  transfers between devices with their start and end apart: 4, of which 2 were waited for; matrix products, arithmetic and copies ran while one was open for 10% of the time, Pallas kernels for 0%

commit v1 on v0

v1 whole, which is shorter than its diff:
```python
import functools
import math

import jax
import jax.numpy as jnp
from jax import lax
from jax.experimental import pallas as pl
from jax.experimental.pallas import tpu as pltpu
from jax.sharding import PartitionSpec as P

MESH = pl.DeviceIdType.MESH
EDGE = 128
HALF = EDGE // 2
CELLS = HALF * HALF
CHUNK = 1024
PER_SAMPLE = CELLS // CHUNK
CHUNKS = 2 * PER_SAMPLE
EARLY = tuple(range(9, 25))
LATE = (25, 26) + tuple(range(9))


def gather_kernel(
    grad_hbm, planes_hbm, w_ref, out_ref, wg_ref,
    held, early, late, planes, groups, carry, share, share_in,
    even, odd, acc, near, mine, far, far_in,
    local_sem, z_send, z_recv, y_send, y_recv, f_send, f_recv,
    halo_send, halo_recv, p_send, p_recv, r_send, r_recv, m_send, m_recv,
):
    slab = lax.axis_index("slab")
    chan = lax.axis_index("chan")
    y, z = chan // 4, chan % 4
    half, spot = slab // 8, slab % 8

    def at(slab_to, chan_to):
        return (slab_to, chan_to)

    along_z = [at(slab, y * 4 + (z + d) % 4) for d in range(1, 4)]
    y_up = at(slab, ((y + 1) % 4) * 4 + z)
    y_down = at(slab, ((y + 3) % 4) * 4 + z)
    near_to = [at(half * 8 + (spot + d) % 8, chan) for d in range(1, 8)]
    mirror = at((1 - half) * 8 + spot, chan)
    before = at(lax.max(slab - 1, 0), chan)
    after = at(lax.min(slab + 1, 15), chan)
    is_edge = (slab == 7) | (slab == 8)
    across = at(15 - slab, chan)

    barrier = pltpu.get_barrier_semaphore()
    peers = along_z + [y_up, y_down] + near_to + [mirror]
    for peer in peers:
        pl.semaphore_signal(barrier, inc=1, device_id=peer, device_id_type=MESH)

    @pl.when(is_edge)
    def _():
        pl.semaphore_signal(barrier, inc=1, device_id=across, device_id_type=MESH)

    own_rows = pl.ds(pl.multiple_of(chan * 16, 16), 16)

    def source(k):
        begin = pl.multiple_of((PER_SAMPLE - 1 - k % PER_SAMPLE) * CHUNK, CHUNK)
        return grad_hbm.at[k // PER_SAMPLE, :, pl.ds(begin, CHUNK)]

    def local(k):
        return pltpu.make_async_copy(source(k), held.at[k, own_rows], local_sem.at[k])

    def remote(src, dst, send, recv, to):
        return pltpu.make_async_remote_copy(
            src_ref=src, dst_ref=dst, send_sem=send, recv_sem=recv, device_id=to, device_id_type=MESH
        )

    def z_copies(k):
        return [
            remote(source(k), held.at[k, own_rows], z_send.at[k, d], z_recv.at[k, d], along_z[d])
            for d in range(3)
        ]

    block = pl.ds(pl.multiple_of(y * 64, 64), 64)
    up_block = pl.ds(pl.multiple_of(((y + 3) % 4) * 64, 64), 32)
    down_block = pl.ds(pl.multiple_of(((y + 1) % 4) * 64 + 32, 32), 32)

    def y_copies(k):
        return [
            remote(held.at[k, block], held.at[k, block], y_send.at[k, 0], y_recv.at[k, 0], y_up),
            remote(held.at[k, block], held.at[k, block], y_send.at[k, 1], y_recv.at[k, 1], y_down),
        ]

    def f_copies(k):
        return [
            remote(held.at[k, up_block], held.at[k, up_block], f_send.at[k, 0], f_recv.at[k, 0], y_up),
            remote(held.at[k, down_block], held.at[k, down_block], f_send.at[k, 1], f_recv.at[k, 1], y_down),
        ]

    halo = remote(planes_hbm.at[1], planes.at[0], halo_send, halo_recv, after)
    load_even = pltpu.make_async_copy(planes_hbm.at[0], planes.at[1], local_sem.at[CHUNKS])
    load_odd = pltpu.make_async_copy(planes_hbm.at[1], planes.at[2], local_sem.at[CHUNKS + 1])

    def share_copy(k):
        return remote(share.at[k], share_in.at[k], p_send.at[k], p_recv.at[k], before)

    load_even.start()
    load_odd.start()
    for k in range(CHUNKS):
        local(k).start()

    @pl.when(is_edge)
    def _():
        pl.semaphore_wait(barrier, len(peers) + 1)

    @pl.when(jnp.logical_not(is_edge))
    def _():
        pl.semaphore_wait(barrier, len(peers))

    for k in range(2):
        for copy in z_copies(k):
            copy.start()

    @pl.when(slab < 15)
    def _():
        halo.start()

    acc[...] = jnp.zeros_like(acc)
    far[...] = jnp.zeros_like(far)
    load_even.wait()
    load_odd.wait()

    lane = lax.broadcasted_iota(jnp.int32, (8, CELLS), 1)
    first_col = lane % HALF == 0
    first_row = lane < HALF

    def view(depth_tap, sample, row_tap, col_tap):
        at_block = (2 * (row_tap != 1) + (col_tap != 1)) * CELLS
        v = planes[depth_tap, sample, :, at_block : at_block + CELLS].astype(jnp.float32)
        amount = (HALF if row_tap == 0 else 0) + (1 if col_tap == 0 else 0)
        if amount:
            v = pltpu.roll(v, amount, 1)
            drop = first_col if col_tap == 0 else first_row
            if col_tap == 0 and row_tap == 0:
                drop = first_col | first_row
            v = jnp.where(drop, 0.0, v)
        return v

    def fill(store, taps):
        for sample in range(2):
            for pair in range((len(taps) + 1) // 2):
                rows = []
                for t in taps[2 * pair : 2 * pair + 2]:
                    rows.append(view(t // 9, sample, (t // 3) % 3, t % 3))
                if len(rows) == 1:
                    rows.append(jnp.zeros_like(rows[0]))
                both = jnp.concatenate(rows, axis=0).astype(jnp.bfloat16)
                for j in range(PER_SAMPLE):
                    store[sample * PER_SAMPLE + PER_SAMPLE - 1 - j, 16 * pair : 16 * pair + 16, :] = both[
                        :, j * CHUNK : (j + 1) * CHUNK
                    ]

    def start_y(k):
        local(k).wait()
        for copy in z_copies(k):
            copy.wait_recv()
        for copy in y_copies(k):
            copy.start()

    def start_f(k):
        for copy in y_copies(k):
            copy.wait_recv()
        for copy in f_copies(k):
            copy.start()

    start_y(0)
    fill(early, EARLY)

    chunk_lane = lax.broadcasted_iota(jnp.int32, (8, CHUNK), 1)
    last_col = chunk_lane % HALF == HALF - 1

    def row_ahead(value, tail):
        wide = jnp.concatenate([value, tail], axis=1)
        return pltpu.roll(wide, CHUNK + 128 - HALF, 1)[:, :CHUNK]

    def col_ahead(value):
        return jnp.where(last_col, 0.0, pltpu.roll(value, CHUNK - 1, 1))

    def phases(depth_tap):
        def fetch(row_tap, col_tap):
            row = 8 * (9 * depth_tap + 3 * row_tap + col_tap)
            return groups[row : row + 8, :]

        def odd_row(col_tap):
            at_carry = 3 * depth_tap + col_tap
            moving = fetch(0, col_tap)
            moved = row_ahead(moving, carry[at_carry])
            carry[at_carry] = moving[:, :128]
            return fetch(2, col_tap) + moved

        found = []
        rows_even = [fetch(1, c) for c in range(3)]
        rows_odd = [odd_row(c) for c in range(3)]
        for rows in (rows_even, rows_odd):
            found.append(rows[1])
            found.append(rows[2] + col_ahead(rows[0]))
        return found

    def lanes_of(k, phase):
        begin = phase * CELLS + (PER_SAMPLE - 1 - k % PER_SAMPLE) * CHUNK
        return pl.ds(pl.multiple_of(begin, CHUNK), CHUNK)

    def late_dot(k):
        term = lax.dot_general(
            held[k], late[k], (((1,), (1,)), ((), ())), preferred_element_type=jnp.float32
        )
        acc[:, :, :, 128:224] += term.reshape(2, 8, 16, 96)

    def finish(k):
        @pl.when(slab < 15)
        def _():
            share_copy(k).wait_recv()

        for phase in range(4):
            value = odd[k % 2, phase]
            inward = jnp.where(slab < 15, share_in[k, phase], 0.0)
            out_ref[1, k // PER_SAMPLE, :, lanes_of(k, phase)] = (value + inward).astype(jnp.bfloat16)

    def step(i, _):
        k = i

        @pl.when(i + 3 < CHUNKS)
        def _():
            for copy in z_copies(i + 3):
                copy.start()

        @pl.when(i + 2 < CHUNKS)
        def _():
            start_y(i + 2)

        @pl.when(i + 1 < CHUNKS)
        def _():
            start_f(i + 1)

        for copy in f_copies(k):
            copy.wait_recv()

        @pl.when(k % PER_SAMPLE == 0)
        def _():
            carry[...] = jnp.zeros_like(carry)

        groups[...] = jnp.dot(w_ref[...], held[k], preferred_element_type=jnp.float32)
        for phase, value in enumerate(phases(0)):
            share[k, phase] = value

        @pl.when(slab > 0)
        def _():
            share_copy(k).start()

        for phase, value in enumerate(phases(1)):
            out_ref[0, k // PER_SAMPLE, :, lanes_of(k, phase)] = value.astype(jnp.bfloat16)
        for phase, value in enumerate(phases(2)):
            odd[k % 2, phase] = value

        term = lax.dot_general(
            held[k], early[k], (((1,), (1,)), ((), ())), preferred_element_type=jnp.float32
        )
        acc[:, :, :, :128] += term.reshape(2, 8, 16, 128)

        @pl.when(k == CHUNKS - 2)
        def _():
            @pl.when(slab > 0)
            def _():
                halo.wait_recv()

            @pl.when(slab == 0)
            def _():
                planes[0] = jnp.zeros_like(planes[0])

            fill(late, LATE)

            def catch_up(n, _):
                late_dot(n)
                return 0

            lax.fori_loop(0, CHUNKS - 2, catch_up, 0)

        @pl.when(k >= CHUNKS - 2)
        def _():
            late_dot(k)

        @pl.when(k >= 1)
        def _():
            finish(k - 1)

        return 0

    for copy in z_copies(2):
        copy.start()
    start_y(1)
    start_f(0)
    lax.fori_loop(0, CHUNKS, step, 0)

    def near_copy(d):
        return remote(acc.at[:, (spot + d + 1) % 8], near.at[d], r_send.at[d], r_recv.at[d], near_to[d])

    for d in range(7):
        near_copy(d).start()
    finish(CHUNKS - 1)
    for d in range(7):
        near_copy(d).wait_recv()
    total = acc[:, spot]
    for d in range(7):
        total = total + near[d]
    mine[...] = total
    far[...] = mine[1 - half]
    last = remote(far, far_in, m_send, m_recv, mirror)
    last.start()
    last.wait_recv()
    scale = 1.0 / math.sqrt(2 * 16 * CELLS)
    wg_ref[...] = (mine[half] + far_in[...]) * scale

    last.wait_send()
    for d in range(7):
        near_copy(d).wait_send()

    def drain(k, _):
        for copy in z_copies(k) + y_copies(k) + f_copies(k):
            copy.wait_send()

        @pl.when(slab > 0)
        def _():
            share_copy(k).wait_send()

        return 0

    lax.fori_loop(0, CHUNKS, drain, 0)

    @pl.when(slab < 15)
    def _():
        halo.wait_send()


def body(activations, out_grad, weights):
    planes = activations.transpose(2, 0, 1, 3)
    grad = out_grad.reshape(2, 16, CELLS)
    w = weights.reshape(216, 256)
    sem = pltpu.SemaphoreType.DMA
    f32, bf16 = jnp.float32, jnp.bfloat16
    any_space = pl.BlockSpec(memory_space=pl.ANY)
    vmem = pl.BlockSpec(memory_space=pltpu.VMEM)
    out, wg = pl.pallas_call(
        gather_kernel,
        out_shape=(
            jax.ShapeDtypeStruct((2, 2, 8, 4 * CELLS), bf16),
            jax.ShapeDtypeStruct((16, 256), f32),
        ),
        in_specs=[any_space, any_space, vmem],
        out_specs=(vmem, vmem),
        scratch_shapes=[
            pltpu.VMEM((CHUNKS, 256, CHUNK), bf16),
            pltpu.VMEM((CHUNKS, 128, CHUNK), bf16),
            pltpu.VMEM((CHUNKS, 96, CHUNK), bf16),
            pltpu.VMEM((3, 2, 8, 4 * CELLS), bf16),
            pltpu.VMEM((216, CHUNK), f32),
            pltpu.VMEM((9, 8, 128), f32),
            pltpu.VMEM((CHUNKS, 4, 8, CHUNK), f32),
            pltpu.VMEM((CHUNKS, 4, 8, CHUNK), f32),
            pltpu.VMEM((1, 8, 128), f32),
            pltpu.VMEM((2, 4, 8, CHUNK), f32),
            pltpu.VMEM((2, 8, 16, 256), f32),
            pltpu.VMEM((7, 2, 16, 256), f32),
            pltpu.VMEM((2, 16, 256), f32),
            pltpu.VMEM((16, 256), f32),
            pltpu.VMEM((16, 256), f32),
            sem((CHUNKS + 2,)),
            sem((CHUNKS, 3)), sem((CHUNKS, 3)),
            sem((CHUNKS, 2)), sem((CHUNKS, 2)),
            sem((CHUNKS, 2)), sem((CHUNKS, 2)),
            sem, sem,
            sem((CHUNKS,)), sem((CHUNKS,)),
            sem((7,)), sem((7,)),
            sem, sem,
        ],
        compiler_params=pltpu.CompilerParams(
            collective_id=0, has_side_effects=True, vmem_limit_bytes=48 * 1024 * 1024
        ),
    )(grad, planes, w)
    input_grad = out.transpose(1, 2, 0, 3)
    taps = wg[:, :216].reshape(16, 27, 8)
    taps = jnp.concatenate([taps[:, 18:], taps[:, :18]], axis=1)
    return input_grad, taps.transpose(1, 2, 0)


def solution(mesh):
    placed = (P(None, "chan", "slab", None), P(None, "chan", "slab", None), P(None, "chan", None))
    return jax.shard_map(
        body,
        mesh=mesh,
        in_specs=placed,
        out_specs=(P(None, "chan", "slab", None), P(None, "chan", "slab")),
        check_vma=False,
    )
```

time: 311 us -> 75.7 us (0.24)
  waiting for transfers between devices: 243 us -> 0 us
  Pallas kernels: 0 us -> 70.1 us
  local copies, waits for them, and re-layouts: 19.5 us -> 4.77 us
  between operations: 14.5 us -> 0.69 us
  matrix products: 13.3 us -> 0 us
  other arithmetic: 11.4 us -> 0.01 us
  starting transfers between devices: 7.15 us -> 0 us
    all_gather x1 -> x0, waiting for transfers between devices: 187 us -> none  [body(): signal = lax.all_gather(source, 'chan', axis=1, tiled=True)]
    pallas_call x0 -> x1, Pallas kernels: none -> 70.1 us  [body(): pl.pallas_call(gather_kernel, out_shape=(jax.ShapeDtypeStruct((2, 2, 8, 4...]
    reduce_scatter x1 -> x0, waiting for transfers between devices: 56.3 us -> none  [body(): lax.psum_scatter(local_grad, 'slab', scatter_dimension=2, tiled=True)]
    dot_general x6 -> x0, matrix products: 13.3 us -> none  [the longest x3 9.15 us: body(): jnp.einsum('tck,bkdp->tbcdp', weights[9 * depth_tap:9 * depth_tap + 9], b...]
    unnamed x35 -> x7, local copies, waits for them, and re-layouts: 11.8 us -> 4.67 us
    ppermute x2 -> x0, starting transfers between devices: 7.07 us -> none  [from_behind(): return lax.ppermute(x, axis, pairs)]
    slice x25 -> x3, local copies, waits for them, and re-layouts: 4.76 us -> 0.11 us  [the longest x1 0.1 us: body(): taps = wg[:, :216].reshape(16, 27, 8)]
    another operation x2 -> x0, other arithmetic: 3.34 us -> none
  transfers between devices with their start and end apart: 4 -> 0, of which waited for: 2 -> 0; matrix products, arithmetic and copies ran while one was open for 10% -> 0% of each run, Pallas kernels for 0% -> 0%
where the time goes in v1:
time: 75.7 us; the launch traced here: 75.6 us
  Pallas kernels  70.1 us (93%)
  local copies, waits for them, and re-layouts  4.77 us (6%)
    pallas_call x1, Pallas kernels, body(): pl.pallas_call(gather_kernel, out_shape=(jax.ShapeDtypeStruct((2, 2, 8, 4...  70.1 us
    unnamed x7, local copies, waits for them, and re-layouts  4.67 us

profile of v1, /device:TPU:1, one launch (start us, length us, event | category | flops | bytes accessed | tf_op | source)
XLA Modules:
  0.0 75.6 jit_solution(6553062603704336267)
XLA Ops:
  0.6 0.0 copy-start
  0.6 0.0 copy-start.1
  0.6 1.9 %copy.14 = bf16[2,8,2,16384]{3,1,0,2:T(8,128)(2,1)S(1)} copy(bf16[2,8,2,16384]{3,2,1,0:T(2,128)(2,1)} %param.3) | data formatting | bytes 2097152 | tf_op args[0]
  2.5 0.0 copy-done
  2.5 0.0 copy-done.1
  2.5 70.1 %shard_map.50 = (bf16[2,2,8,16384]{3,2,1,0:T(8,128)(2,1)S(1)}, f32[16,256]{1,0:T(8,128)S(1)}) custom-call(bf16[2,16,4096]{2,1,0:T(8,128)(2,1)S(1)} %bitcast.12, bf16[2,2,8,16384]{3,2,1,0:T(8,128)(2,1)S(1)} %bitcast.10, bf16[216,256]{1,0:T(8,128)(2,1)S(1)} %bitcast.13), custom_call_target="tpu_custom_call" | custom-call | tf_op jit(solution)/shard_map/pallas_call | solution.py:344
  72.7 2.1 %copy.11 = bf16[2,8,2,16384]{3,2,1,0:T(2,128)(2,1)} copy(bf16[2,8,2,16384]{3,1,0,2:T(8,128)(2,1)S(1)} %bitcast.11) | data formatting | bytes 2097152
  74.7 0.1 copy.10
  74.9 0.8 copy.12
  (3 shorter events, 0.0 us)
Async XLA Ops:
  0.6 1.9 %copy-start = (bf16[2,16,1,4096]{3,1,2,0:T(8,128)(2,1)S(1)}, bf16[2,16,1,4096]{3,1,2,0:T(8,128)(2,1)}, u32[]{:S(2)}) copy-start(bf16[2,16,1,4096]{3,1,2,0:T(8,128)(2,1)} %param.4) | copy-start | bytes 786436
  0.6 1.9 %copy-start.1 = (bf16[27,8,256]{2,1,0:T(8,128)(2,1)S(1)}, bf16[27,8,256]{2,1,0:T(8,128)(2,1)}, u32[]{:S(2)}) copy-start(bf16[27,8,256]{2,1,0:T(8,128)(2,1)} %param.5) | copy-start | bytes 331780

commit v2 on v1

--- a/solution.py
+++ b/solution.py
@@ -16,15 +16,17 @@
 PER_SAMPLE = CELLS // CHUNK
 CHUNKS = 2 * PER_SAMPLE
 EARLY = tuple(range(9, 25))
+HALO_AT = 4
 LATE = (25, 26) + tuple(range(9))
 
 
 def gather_kernel(
     grad_hbm, planes_hbm, w_ref, out_ref, wg_ref,
     held, early, late, planes, groups, carry, share, share_in,
-    even, odd, acc, near, mine, far, far_in,
+    odd, acc, pair_in, paired, near, mine, far, far_in, relay, halo_relay,
     local_sem, z_send, z_recv, y_send, y_recv, f_send, f_recv,
-    halo_send, halo_recv, p_send, p_recv, r_send, r_recv, m_send, m_recv,
+    halo_send, halo_recv, p_send, p_recv, q_send, q_recv, h_send, h_recv,
+    c_send, c_recv, r_send, r_recv, m_send, m_recv,
 ):
     slab = lax.axis_index("slab")
     chan = lax.axis_index("chan")
@@ -37,21 +39,42 @@
     along_z = [at(slab, y * 4 + (z + d) % 4) for d in range(1, 4)]
     y_up = at(slab, ((y + 1) % 4) * 4 + z)
     y_down = at(slab, ((y + 3) % 4) * 4 + z)
+    column, core = spot // 2, spot % 2
     near_to = [at(half * 8 + (spot + d) % 8, chan) for d in range(1, 8)]
+    pair = at(slab + 1 - 2 * core, chan)
+    along_x = [at(half * 8 + (spot + 2 * d) % 8, chan) for d in range(1, 4)]
     mirror = at((1 - half) * 8 + spot, chan)
     before = at(lax.max(slab - 1, 0), chan)
     after = at(lax.min(slab + 1, 15), chan)
-    is_edge = (slab == 7) | (slab == 8)
-    across = at(15 - slab, chan)
+    low_side = (slab < 6) & (core == 1)
+    high_side = (slab > 8) & (core == 0)
 
     barrier = pltpu.get_barrier_semaphore()
     peers = along_z + [y_up, y_down] + near_to + [mirror]
+
+    def greet(peer):
+        pl.semaphore_signal(barrier, inc=1, device_id=peer, device_id_type=MESH)
+
     for peer in peers:
-        pl.semaphore_signal(barrier, inc=1, device_id=peer, device_id_type=MESH)
-
-    @pl.when(is_edge)
-    def _():
-        pl.semaphore_signal(barrier, inc=1, device_id=across, device_id_type=MESH)
+        greet(peer)
+
+    @pl.when(slab == 7)
+    def _():
+        for q in range(4):
+            greet(at(8 + 2 * q, chan))
+
+    @pl.when(slab == 8)
+    def _():
+        for q in range(4):
+            greet(at(1 + 2 * q, chan))
+
+    @pl.when(low_side)
+    def _():
+        greet(at(8, chan))
+
+    @pl.when(high_side)
+    def _():
+        greet(at(7, chan))
 
     own_rows = pl.ds(pl.multiple_of(chan * 16, 16), 16)
 
@@ -89,36 +112,90 @@
             remote(held.at[k, down_block], held.at[k, down_block], f_send.at[k, 1], f_recv.at[k, 1], y_down),
         ]
 
-    halo = remote(planes_hbm.at[1], planes.at[0], halo_send, halo_recv, after)
+    halo = remote(planes_hbm.at[1], planes.at[0], halo_send.at[0], halo_recv.at[0], after)
+
+    def quarter(q):
+        return pl.ds(pl.multiple_of(q * CELLS, CELLS), CELLS)
+
+    def halo_out(q):
+        if q == 3:
+            return remote(
+                planes_hbm.at[1, :, :, quarter(3)], planes.at[0, :, :, quarter(3)],
+                halo_send.at[3], halo_recv.at[3], at(8, chan),
+            )
+        return remote(
+            planes_hbm.at[1, :, :, quarter(q)], halo_relay,
+            halo_send.at[q], h_recv, at(1 + 2 * q, chan),
+        )
+
+    halo_on = remote(
+        halo_relay, planes.at[0, :, :, quarter(column)], h_send, halo_recv.at[column], at(8, chan)
+    )
     load_even = pltpu.make_async_copy(planes_hbm.at[0], planes.at[1], local_sem.at[CHUNKS])
     load_odd = pltpu.make_async_copy(planes_hbm.at[1], planes.at[2], local_sem.at[CHUNKS + 1])
 
-    def share_copy(k):
-        return remote(share.at[k], share_in.at[k], p_send.at[k], p_recv.at[k], before)
+    def share_copy(k, q):
+        return remote(share.at[k, q], share_in.at[k, q], p_send.at[k, q], p_recv.at[k, q], before)
+
+    def share_out(k, q):
+        if q == 0:
+            return share_copy(k, 0)
+        return remote(share.at[k, q], relay.at[k], p_send.at[k, q], q_recv.at[k], at(8 + 2 * q, chan))
+
+    def share_on(k):
+        return remote(relay.at[k], share_in.at[k, column], q_send.at[k], p_recv.at[k, column], at(7, chan))
+
+    def send_share(k):
+        @pl.when((slab > 0) & (slab != 8))
+        def _():
+            for q in range(4):
+                share_copy(k, q).start()
+
+        @pl.when(slab == 8)
+        def _():
+            for q in (1, 2, 3, 0):
+                share_out(k, q).start()
+
+    def pass_share(k):
+        @pl.when(high_side)
+        def _():
+            share_out(k, 1).wait_recv()
+            share_on(k).start()
 
     load_even.start()
     load_odd.start()
     for k in range(CHUNKS):
         local(k).start()
 
+    is_edge = (slab == 7) | (slab == 8)
+    is_side = low_side | high_side
+
     @pl.when(is_edge)
     def _():
+        pl.semaphore_wait(barrier, len(peers) + 4)
+
+    @pl.when(is_side)
+    def _():
         pl.semaphore_wait(barrier, len(peers) + 1)
 
-    @pl.when(jnp.logical_not(is_edge))
+    @pl.when(jnp.logical_not(is_edge | is_side))
     def _():
         pl.semaphore_wait(barrier, len(peers))
 
-    for k in range(2):
+    for k in range(CHUNKS):
         for copy in z_copies(k):
             copy.start()
 
-    @pl.when(slab < 15)
+    @pl.when((slab < 15) & (slab != 7))
     def _():
         halo.start()
 
+    @pl.when(slab == 7)
+    def _():
+        for q in range(4):
+            halo_out(q).start()
+
     acc[...] = jnp.zeros_like(acc)
-    far[...] = jnp.zeros_like(far)
     load_even.wait()
     load_odd.wait()
 
@@ -206,37 +283,26 @@
         term = lax.dot_general(
             held[k], late[k], (((1,), (1,)), ((), ())), preferred_element_type=jnp.float32
         )
-        acc[:, :, :, 128:224] += term.reshape(2, 8, 16, 96)
+        acc[:, :, :, :, 128:224] += term.reshape(2, 4, 2, 16, 96)
 
     def finish(k):
         @pl.when(slab < 15)
         def _():
-            share_copy(k).wait_recv()
+            for q in range(4):
+                share_copy(k, q).wait_recv()
 
         for phase in range(4):
             value = odd[k % 2, phase]
             inward = jnp.where(slab < 15, share_in[k, phase], 0.0)
             out_ref[1, k // PER_SAMPLE, :, lanes_of(k, phase)] = (value + inward).astype(jnp.bfloat16)
 
-    def step(i, _):
-        k = i
-
-        @pl.when(i + 3 < CHUNKS)
-        def _():
-            for copy in z_copies(i + 3):
-                copy.start()
-
-        @pl.when(i + 2 < CHUNKS)
-        def _():
-            start_y(i + 2)
-
-        @pl.when(i + 1 < CHUNKS)
-        def _():
-            start_f(i + 1)
-
-        for copy in f_copies(k):
-            copy.wait_recv()
-
+    def early_dot(k):
+        term = lax.dot_general(
+            held[k], early[k], (((1,), (1,)), ((), ())), preferred_element_type=jnp.float32
+        )
+        acc[:, :, :, :, :128] += term.reshape(2, 4, 2, 16, 128)
+
+    def input_part(k):
         @pl.when(k % PER_SAMPLE == 0)
         def _():
             carry[...] = jnp.zeros_like(carry)
@@ -244,26 +310,39 @@
         groups[...] = jnp.dot(w_ref[...], held[k], preferred_element_type=jnp.float32)
         for phase, value in enumerate(phases(0)):
             share[k, phase] = value
-
-        @pl.when(slab > 0)
-        def _():
-            share_copy(k).start()
-
+        send_share(k)
         for phase, value in enumerate(phases(1)):
             out_ref[0, k // PER_SAMPLE, :, lanes_of(k, phase)] = value.astype(jnp.bfloat16)
         for phase, value in enumerate(phases(2)):
             odd[k % 2, phase] = value
 
-        term = lax.dot_general(
-            held[k], early[k], (((1,), (1,)), ((), ())), preferred_element_type=jnp.float32
-        )
-        acc[:, :, :, :128] += term.reshape(2, 8, 16, 128)
-
-        @pl.when(k == CHUNKS - 2)
-        def _():
-            @pl.when(slab > 0)
+    def receive(k):
+        for copy in f_copies(k):
+            copy.wait_recv()
+
+    def step(k, _):
+        @pl.when(k + 2 < CHUNKS)
+        def _():
+            start_y(k + 2)
+
+        start_f(k + 1)
+        receive(k)
+        input_part(k)
+        early_dot(k)
+
+        @pl.when(k == HALO_AT)
+        def _():
+            @pl.when((slab > 0) & (slab != 8))
             def _():
                 halo.wait_recv()
+
+            @pl.when(slab == 8)
+            def _():
+                for q in range(4):
+                    pltpu.make_async_remote_copy(
+                        src_ref=planes.at[0, :, :, quarter(q)], dst_ref=planes.at[0, :, :, quarter(q)],
+                        send_sem=h_send, recv_sem=halo_recv.at[q], device_id=mirror, device_id_type=MESH,
+                    ).wait_recv()
 
             @pl.when(slab == 0)
             def _():
@@ -275,45 +354,62 @@
                 late_dot(n)
                 return 0
 
-            lax.fori_loop(0, CHUNKS - 2, catch_up, 0)
-
-        @pl.when(k >= CHUNKS - 2)
+            lax.fori_loop(0, HALO_AT, catch_up, 0)
+
+        @pl.when(k == 1)
+        def _():
+            @pl.when(low_side)
+            def _():
+                halo_out(0).wait_recv()
+                halo_on.start()
+
+        @pl.when(k >= HALO_AT)
         def _():
             late_dot(k)
 
         @pl.when(k >= 1)
         def _():
+            pass_share(k - 1)
             finish(k - 1)
 
         return 0
 
-    for copy in z_copies(2):
-        copy.start()
     start_y(1)
     start_f(0)
-    lax.fori_loop(0, CHUNKS, step, 0)
+    lax.fori_loop(0, CHUNKS - 1, step, 0)
+
+    end = CHUNKS - 1
+    pair_copy = remote(acc.at[:, :, 1 - core], pair_in, c_send, c_recv, pair)
 
     def near_copy(d):
-        return remote(acc.at[:, (spot + d + 1) % 8], near.at[d], r_send.at[d], r_recv.at[d], near_to[d])
-
-    for d in range(7):
+        return remote(paired.at[:, (column + d + 1) % 4], near.at[d], r_send.at[d], r_recv.at[d], along_x[d])
+
+    receive(end)
+    early_dot(end)
+    late_dot(end)
+    pair_copy.start()
+    input_part(end)
+    pass_share(end - 1)
+    pair_copy.wait_recv()
+    paired[...] = acc[:, :, core] + pair_in[...]
+    for d in range(3):
         near_copy(d).start()
-    finish(CHUNKS - 1)
-    for d in range(7):
+    pass_share(end)
+    finish(end - 1)
+    for d in range(3):
         near_copy(d).wait_recv()
-    total = acc[:, spot]
-    for d in range(7):
-        total = total + near[d]
-    mine[...] = total
+    mine[...] = paired[:, column] + near[0] + near[1] + near[2]
     far[...] = mine[1 - half]
     last = remote(far, far_in, m_send, m_recv, mirror)
     last.start()
+    finish(end)
     last.wait_recv()
     scale = 1.0 / math.sqrt(2 * 16 * CELLS)
     wg_ref[...] = (mine[half] + far_in[...]) * scale
 
     last.wait_send()
-    for d in range(7):
+    pair_copy.wait_send()
+    for d in range(3):
         near_copy(d).wait_send()
 
     def drain(k, _):
@@ -322,15 +418,29 @@
 
         @pl.when(slab > 0)
         def _():
-            share_copy(k).wait_send()
+            for q in range(4):
+                share_copy(k, q).wait_send()
+
+        @pl.when(high_side)
+        def _():
+            share_on(k).wait_send()
 
         return 0
 
     lax.fori_loop(0, CHUNKS, drain, 0)
 
-    @pl.when(slab < 15)
+    @pl.when((slab < 15) & (slab != 7))
     def _():
         halo.wait_send()
+
+    @pl.when(slab == 7)
+    def _():
+        for q in range(4):
+            halo_out(q).wait_send()
+
+    @pl.when(low_side)
+    def _():
+        halo_on.wait_send()
 
 
 def body(activations, out_grad, weights):
@@ -358,20 +468,26 @@
             pltpu.VMEM((9, 8, 128), f32),
             pltpu.VMEM((CHUNKS, 4, 8, CHUNK), f32),
             pltpu.VMEM((CHUNKS, 4, 8, CHUNK), f32),
-            pltpu.VMEM((1, 8, 128), f32),
             pltpu.VMEM((2, 4, 8, CHUNK), f32),
-            pltpu.VMEM((2, 8, 16, 256), f32),
-            pltpu.VMEM((7, 2, 16, 256), f32),
+            pltpu.VMEM((2, 4, 2, 16, 256), f32),
+            pltpu.VMEM((2, 4, 16, 256), f32),
+            pltpu.VMEM((2, 4, 16, 256), f32),
+            pltpu.VMEM((3, 2, 16, 256), f32),
             pltpu.VMEM((2, 16, 256), f32),
             pltpu.VMEM((16, 256), f32),
             pltpu.VMEM((16, 256), f32),
+            pltpu.VMEM((CHUNKS, 8, CHUNK), f32),
+            pltpu.VMEM((2, 8, CELLS), bf16),
             sem((CHUNKS + 2,)),
             sem((CHUNKS, 3)), sem((CHUNKS, 3)),
             sem((CHUNKS, 2)), sem((CHUNKS, 2)),
             sem((CHUNKS, 2)), sem((CHUNKS, 2)),
+            sem((4,)), sem((4,)),
+            sem((CHUNKS, 4)), sem((CHUNKS, 4)),
+            sem((CHUNKS,)), sem((CHUNKS,)),
             sem, sem,
-            sem((CHUNKS,)), sem((CHUNKS,)),
-            sem((7,)), sem((7,)),
+            sem, sem,
+            sem((3,)), sem((3,)),
             sem, sem,
         ],
         compiler_params=pltpu.CompilerParams(

time: 75.7 us -> 73.7 us (0.974); the launches traced: 75.6 us -> 72.2 us
  Pallas kernels: 70.1 us -> 66.8 us
    pallas_call x1, Pallas kernels: 70.1 us -> 66.8 us  [body(): pl.pallas_call(gather_kernel, out_shape=(jax.ShapeDtypeStruct((2, 2, 8, 4...]
where the time goes in v2:
time: 73.7 us; the launch traced here: 72.2 us
  Pallas kernels  66.8 us (91%)
  local copies, waits for them, and re-layouts  4.77 us (6%)
    pallas_call x1, Pallas kernels, body(): pl.pallas_call(gather_kernel, out_shape=(jax.ShapeDtypeStruct((2, 2, 8, 4...  66.8 us
    unnamed x7, local copies, waits for them, and re-layouts  4.67 us

profile of v2, /device:TPU:1, one launch (start us, length us, event | category | flops | bytes accessed | tf_op | source)
XLA Modules:
  0.0 72.2 jit_solution(8594525207722177164)
XLA Ops:
  0.6 0.0 copy-start
  0.6 0.0 copy-start.1
  0.6 1.9 %copy.14 = bf16[2,8,2,16384]{3,1,0,2:T(8,128)(2,1)S(1)} copy(bf16[2,8,2,16384]{3,2,1,0:T(2,128)(2,1)} %param.3) | data formatting | bytes 2097152 | tf_op args[0]
  2.5 0.0 copy-done
  2.5 0.0 copy-done.1
  2.5 66.8 %shard_map.50 = (bf16[2,2,8,16384]{3,2,1,0:T(8,128)(2,1)S(1)}, f32[16,256]{1,0:T(8,128)S(1)}) custom-call(bf16[2,16,4096]{2,1,0:T(8,128)(2,1)S(1)} %bitcast.12, bf16[2,2,8,16384]{3,2,1,0:T(8,128)(2,1)S(1)} %bitcast.10, bf16[216,256]{1,0:T(8,128)(2,1)S(1)} %bitcast.13), custom_call_target="tpu_custom_call" | custom-call | tf_op jit(solution)/shard_map/pallas_call | solution.py:454
  69.3 2.1 %copy.11 = bf16[2,8,2,16384]{3,2,1,0:T(2,128)(2,1)} copy(bf16[2,8,2,16384]{3,1,0,2:T(8,128)(2,1)S(1)} %bitcast.11) | data formatting | bytes 2097152
  71.3 0.1 copy.10
  71.5 0.8 %copy.12 = f32[27,8,16]{0,2,1:T(8,128)} copy(f32[27,8,16]{2,1,0:T(8,128)S(1)} %maximum_bitcast_fusion) | data formatting | bytes 27648
  (3 shorter events, 0.0 us)
Async XLA Ops:
  0.6 1.9 %copy-start = (bf16[2,16,1,4096]{3,1,2,0:T(8,128)(2,1)S(1)}, bf16[2,16,1,4096]{3,1,2,0:T(8,128)(2,1)}, u32[]{:S(2)}) copy-start(bf16[2,16,1,4096]{3,1,2,0:T(8,128)(2,1)} %param.4) | copy-start | bytes 786436
  0.6 1.9 %copy-start.1 = (bf16[27,8,256]{2,1,0:T(8,128)(2,1)S(1)}, bf16[27,8,256]{2,1,0:T(8,128)(2,1)}, u32[]{:S(2)}) copy-start(bf16[27,8,256]{2,1,0:T(8,128)(2,1)} %param.5) | copy-start | bytes 331780

commit v3 on v2

--- a/solution.py
+++ b/solution.py
@@ -17,16 +17,17 @@
 CHUNKS = 2 * PER_SAMPLE
 EARLY = tuple(range(9, 25))
 HALO_AT = 4
+CROSS = CHUNKS - 1
 LATE = (25, 26) + tuple(range(9))
 
 
 def gather_kernel(
     grad_hbm, planes_hbm, w_ref, out_ref, wg_ref,
     held, early, late, planes, groups, carry, share, share_in,
-    odd, acc, pair_in, paired, near, mine, far, far_in, relay, halo_relay,
+    odd, acc, pair_in, paired, near, relay, halo_relay,
     local_sem, z_send, z_recv, y_send, y_recv, f_send, f_recv,
     halo_send, halo_recv, p_send, p_recv, q_send, q_recv, h_send, h_recv,
-    c_send, c_recv, r_send, r_recv, m_send, m_recv,
+    c_send, c_recv, r_send, r_recv, by_send, by_recv, bf_send, bf_recv, bz_send, bz_recv,
 ):
     slab = lax.axis_index("slab")
     chan = lax.axis_index("chan")
@@ -42,7 +43,14 @@
     column, core = spot // 2, spot % 2
     near_to = [at(half * 8 + (spot + d) % 8, chan) for d in range(1, 8)]
     pair = at(slab + 1 - 2 * core, chan)
-    along_x = [at(half * 8 + (spot + 2 * d) % 8, chan) for d in range(1, 4)]
+    place = half * 4 + column
+
+    def core_peer(d):
+        to = (place + d) % 8
+        return at((to // 4) * 8 + (to % 4) * 2 + core, chan)
+
+    spread_to = [core_peer(d) for d in range(1, 8)]
+    across = [at((1 - half) * 8 + (spot + 2 * d) % 8, chan) for d in range(4)]
     mirror = at((1 - half) * 8 + spot, chan)
     before = at(lax.max(slab - 1, 0), chan)
     after = at(lax.min(slab + 1, 15), chan)
@@ -50,7 +58,7 @@
     high_side = (slab > 8) & (core == 0)
 
     barrier = pltpu.get_barrier_semaphore()
-    peers = along_z + [y_up, y_down] + near_to + [mirror]
+    peers = along_z + [y_up, y_down] + near_to + across
 
     def greet(peer):
         pl.semaphore_signal(barrier, inc=1, device_id=peer, device_id_type=MESH)
@@ -75,15 +83,13 @@
     @pl.when(high_side)
     def _():
         greet(at(7, chan))
-
-    own_rows = pl.ds(pl.multiple_of(chan * 16, 16), 16)
 
     def source(k):
         begin = pl.multiple_of((PER_SAMPLE - 1 - k % PER_SAMPLE) * CHUNK, CHUNK)
         return grad_hbm.at[k // PER_SAMPLE, :, pl.ds(begin, CHUNK)]
 
     def local(k):
-        return pltpu.make_async_copy(source(k), held.at[k, own_rows], local_sem.at[k])
+        return pltpu.make_async_copy(source(k), held.at[k, y, z], local_sem.at[k])
 
     def remote(src, dst, send, recv, to):
         return pltpu.make_async_remote_copy(
@@ -92,25 +98,77 @@
 
     def z_copies(k):
         return [
-            remote(source(k), held.at[k, own_rows], z_send.at[k, d], z_recv.at[k, d], along_z[d])
+            remote(source(k), held.at[k, y, z], z_send.at[k, d], z_recv.at[k, d], along_z[d])
             for d in range(3)
         ]
 
-    block = pl.ds(pl.multiple_of(y * 64, 64), 64)
-    up_block = pl.ds(pl.multiple_of(((y + 3) % 4) * 64, 64), 32)
-    down_block = pl.ds(pl.multiple_of(((y + 1) % 4) * 64 + 32, 32), 32)
+    low, high = (y + 3) % 4, (y + 1) % 4
 
     def y_copies(k):
+        block = held.at[k, y]
         return [
-            remote(held.at[k, block], held.at[k, block], y_send.at[k, 0], y_recv.at[k, 0], y_up),
-            remote(held.at[k, block], held.at[k, block], y_send.at[k, 1], y_recv.at[k, 1], y_down),
+            remote(block, block, y_send.at[k, 0], y_recv.at[k, 0], y_up),
+            remote(block, block, y_send.at[k, 1], y_recv.at[k, 1], y_down),
         ]
 
     def f_copies(k):
+        from_low, from_high = held.at[k, low, pl.ds(0, 2)], held.at[k, high, pl.ds(2, 2)]
         return [
-            remote(held.at[k, up_block], held.at[k, up_block], f_send.at[k, 0], f_recv.at[k, 0], y_up),
-            remote(held.at[k, down_block], held.at[k, down_block], f_send.at[k, 1], f_recv.at[k, 1], y_down),
+            remote(from_low, from_low, f_send.at[k, 0], f_recv.at[k, 0], y_up),
+            remote(from_high, from_high, f_send.at[k, 1], f_recv.at[k, 1], y_down),
         ]
+
+    def cross_y():
+        return [
+            remote(source(CROSS), held.at[CROSS, y, z], by_send.at[0], by_recv.at[0], y_up),
+            remote(source(CROSS), held.at[CROSS, y, z], by_send.at[1], by_recv.at[1], y_down),
+        ]
+
+    def cross_f():
+        from_low = held.at[CROSS, low, z, :, pl.ds(0, CHUNK // 2)]
+        from_high = held.at[CROSS, high, z, :, pl.ds(CHUNK // 2, CHUNK // 2)]
+        return [
+            remote(from_low, from_low, bf_send.at[0], bf_recv.at[0], y_up),
+            remote(from_high, from_high, bf_send.at[1], bf_recv.at[1], y_down),
+        ]
+
+    z_up = at(slab, y * 4 + lax.min(z + 1, 3))
+    z_down = at(slab, y * 4 + lax.max(z - 1, 0))
+
+    def cross_up(hop):
+        piece = held.at[CROSS, :, lax.max(z - hop, 0)]
+        return remote(piece, piece, bz_send.at[0, hop], bz_recv.at[0, hop], z_up)
+
+    def cross_down(hop):
+        piece = held.at[CROSS, :, lax.min(z + hop, 3)]
+        return remote(piece, piece, bz_send.at[1, hop], bz_recv.at[1, hop], z_down)
+
+    def cross_send(hop):
+        @pl.when((z < 3) & (z >= hop))
+        def _():
+            cross_up(hop).start()
+
+        @pl.when((z > 0) & (z + hop <= 3))
+        def _():
+            cross_down(hop).start()
+
+    def cross_wait_send(hop):
+        @pl.when((z < 3) & (z >= hop))
+        def _():
+            cross_up(hop).wait_send()
+
+        @pl.when((z > 0) & (z + hop <= 3))
+        def _():
+            cross_down(hop).wait_send()
+
+    def cross_recv(hop):
+        @pl.when(z > hop)
+        def _():
+            cross_up(hop).wait_recv()
+
+        @pl.when(z + hop < 3)
+        def _():
+            cross_down(hop).wait_recv()
 
     halo = remote(planes_hbm.at[1], planes.at[0], halo_send.at[0], halo_recv.at[0], after)
 
@@ -182,7 +240,9 @@
     def _():
         pl.semaphore_wait(barrier, len(peers))
 
-    for k in range(CHUNKS):
+    for copy in cross_y():
+        copy.start()
+    for k in range(4):
         for copy in z_copies(k):
             copy.start()
 
@@ -242,8 +302,16 @@
         for copy in f_copies(k):
             copy.start()
 
+    for copy in cross_y():
+        copy.wait_recv()
+    for copy in cross_f():
+        copy.start()
     start_y(0)
     fill(early, EARLY)
+    local(CROSS).wait()
+    for copy in cross_f():
+        copy.wait_recv()
+    cross_send(0)
 
     chunk_lane = lax.broadcasted_iota(jnp.int32, (8, CHUNK), 1)
     last_col = chunk_lane % HALF == HALF - 1
@@ -281,7 +349,7 @@
 
     def late_dot(k):
         term = lax.dot_general(
-            held[k], late[k], (((1,), (1,)), ((), ())), preferred_element_type=jnp.float32
+            held[k].reshape(256, CHUNK), late[k], (((1,), (1,)), ((), ())), preferred_element_type=jnp.float32
         )
         acc[:, :, :, :, 128:224] += term.reshape(2, 4, 2, 16, 96)
 
@@ -298,7 +366,7 @@
 
     def early_dot(k):
         term = lax.dot_general(
-            held[k], early[k], (((1,), (1,)), ((), ())), preferred_element_type=jnp.float32
+            held[k].reshape(256, CHUNK), early[k], (((1,), (1,)), ((), ())), preferred_element_type=jnp.float32
         )
         acc[:, :, :, :, :128] += term.reshape(2, 4, 2, 16, 128)
 
@@ -307,7 +375,7 @@
         def _():
             carry[...] = jnp.zeros_like(carry)
 
-        groups[...] = jnp.dot(w_ref[...], held[k], preferred_element_type=jnp.float32)
+        groups[...] = jnp.dot(w_ref[...], held[k].reshape(256, CHUNK), preferred_element_type=jnp.float32)
         for phase, value in enumerate(phases(0)):
             share[k, phase] = value
         send_share(k)
@@ -321,7 +389,12 @@
             copy.wait_recv()
 
     def step(k, _):
-        @pl.when(k + 2 < CHUNKS)
+        @pl.when(k + 4 < CROSS)
+        def _():
+            for copy in z_copies(k + 4):
+                copy.start()
+
+        @pl.when(k + 2 < CROSS)
         def _():
             start_y(k + 2)
 
@@ -358,6 +431,16 @@
 
         @pl.when(k == 1)
         def _():
+            cross_recv(0)
+            cross_send(1)
+
+        @pl.when(k == 3)
+        def _():
+            cross_recv(1)
+            cross_send(2)
+
+        @pl.when(k == 1)
+        def _():
             @pl.when(low_side)
             def _():
                 halo_out(0).wait_recv()
@@ -376,45 +459,54 @@
 
     start_y(1)
     start_f(0)
-    lax.fori_loop(0, CHUNKS - 1, step, 0)
-
-    end = CHUNKS - 1
+    lax.fori_loop(0, CROSS - 1, step, 0)
+
+    tail = CROSS - 1
     pair_copy = remote(acc.at[:, :, 1 - core], pair_in, c_send, c_recv, pair)
 
-    def near_copy(d):
-        return remote(paired.at[:, (column + d + 1) % 4], near.at[d], r_send.at[d], r_recv.at[d], along_x[d])
-
-    receive(end)
-    early_dot(end)
-    late_dot(end)
+    def spread(d):
+        to = (place + d + 1) % 8
+        return remote(paired.at[to // 4, to % 4], near.at[d], r_send.at[d], r_recv.at[d], spread_to[d])
+
+    cross_recv(2)
+    early_dot(CROSS)
+    late_dot(CROSS)
+    receive(tail)
+    early_dot(tail)
+    late_dot(tail)
     pair_copy.start()
-    input_part(end)
-    pass_share(end - 1)
+    input_part(tail)
+    pass_share(tail - 1)
     pair_copy.wait_recv()
     paired[...] = acc[:, :, core] + pair_in[...]
-    for d in range(3):
-        near_copy(d).start()
-    pass_share(end)
-    finish(end - 1)
-    for d in range(3):
-        near_copy(d).wait_recv()
-    mine[...] = paired[:, column] + near[0] + near[1] + near[2]
-    far[...] = mine[1 - half]
-    last = remote(far, far_in, m_send, m_recv, mirror)
-    last.start()
-    finish(end)
-    last.wait_recv()
+    for d in range(7):
+        spread(d).start()
+    finish(tail - 1)
+    input_part(CROSS)
+    pass_share(tail)
+    finish(tail)
+    pass_share(CROSS)
+    finish(CROSS)
+    total = paired[half, column]
+    for d in range(7):
+        spread(d).wait_recv()
+        total = total + near[d]
     scale = 1.0 / math.sqrt(2 * 16 * CELLS)
-    wg_ref[...] = (mine[half] + far_in[...]) * scale
-
-    last.wait_send()
+    wg_ref[...] = total * scale
+
     pair_copy.wait_send()
-    for d in range(3):
-        near_copy(d).wait_send()
+    for d in range(7):
+        spread(d).wait_send()
+    for copy in cross_y() + cross_f():
+        copy.wait_send()
+    for hop in range(3):
+        cross_wait_send(hop)
 
     def drain(k, _):
-        for copy in z_copies(k) + y_copies(k) + f_copies(k):
-            copy.wait_send()
+        @pl.when(k < CROSS)
+        def _():
+            for copy in z_copies(k) + y_copies(k) + f_copies(k):
+                copy.wait_send()
 
         @pl.when(slab > 0)
         def _():
@@ -460,7 +552,7 @@
         in_specs=[any_space, any_space, vmem],
         out_specs=(vmem, vmem),
         scratch_shapes=[
-            pltpu.VMEM((CHUNKS, 256, CHUNK), bf16),
+            pltpu.VMEM((CHUNKS, 4, 4, 16, CHUNK), bf16),
             pltpu.VMEM((CHUNKS, 128, CHUNK), bf16),
             pltpu.VMEM((CHUNKS, 96, CHUNK), bf16),
             pltpu.VMEM((3, 2, 8, 4 * CELLS), bf16),
@@ -472,10 +564,7 @@
             pltpu.VMEM((2, 4, 2, 16, 256), f32),
             pltpu.VMEM((2, 4, 16, 256), f32),
             pltpu.VMEM((2, 4, 16, 256), f32),
-            pltpu.VMEM((3, 2, 16, 256), f32),
-            pltpu.VMEM((2, 16, 256), f32),
-            pltpu.VMEM((16, 256), f32),
-            pltpu.VMEM((16, 256), f32),
+            pltpu.VMEM((7, 16, 256), f32),
             pltpu.VMEM((CHUNKS, 8, CHUNK), f32),
             pltpu.VMEM((2, 8, CELLS), bf16),
             sem((CHUNKS + 2,)),
@@ -487,8 +576,10 @@
             sem((CHUNKS,)), sem((CHUNKS,)),
             sem, sem,
             sem, sem,
-            sem((3,)), sem((3,)),
-            sem, sem,
+            sem((7,)), sem((7,)),
+            sem((2,)), sem((2,)),
+            sem((2,)), sem((2,)),
+            sem((2, 3)), sem((2, 3)),
         ],
         compiler_params=pltpu.CompilerParams(
             collective_id=0, has_side_effects=True, vmem_limit_bytes=48 * 1024 * 1024

time: 73.7 us -> 67.5 us (0.916); the launches traced: 72.2 us -> 67.4 us
  Pallas kernels: 66.8 us -> 61.9 us
    pallas_call x1, Pallas kernels: 66.8 us -> 61.9 us  [body(): pl.pallas_call(gather_kernel, out_shape=(jax.ShapeDtypeStruct((2, 2, 8, 4...]
where the time goes in v3:
time: 67.5 us; the launch traced here: 67.4 us
  Pallas kernels  61.9 us (92%)
  local copies, waits for them, and re-layouts  4.77 us (7%)
  between operations  0.69 us (1%)
    pallas_call x1, Pallas kernels, body(): pl.pallas_call(gather_kernel, out_shape=(jax.ShapeDtypeStruct((2, 2, 8, 4...  61.9 us
    unnamed x7, local copies, waits for them, and re-layouts  4.67 us

profile of v3, /device:TPU:1, one launch (start us, length us, event | category | flops | bytes accessed | tf_op | source)
XLA Modules:
  0.0 67.4 jit_solution(5803828536197162878)
XLA Ops:
  0.6 0.0 copy-start
  0.6 0.0 copy-start.1
  0.6 1.9 %copy.14 = bf16[2,8,2,16384]{3,1,0,2:T(8,128)(2,1)S(1)} copy(bf16[2,8,2,16384]{3,2,1,0:T(2,128)(2,1)} %param.3) | data formatting | bytes 2097152 | tf_op args[0]
  2.5 0.0 copy-done
  2.5 0.0 copy-done.1
  2.5 61.9 %shard_map.50 = (bf16[2,2,8,16384]{3,2,1,0:T(8,128)(2,1)S(1)}, f32[16,256]{1,0:T(8,128)S(1)}) custom-call(bf16[2,16,4096]{2,1,0:T(8,128)(2,1)S(1)} %bitcast.12, bf16[2,2,8,16384]{3,2,1,0:T(8,128)(2,1)S(1)} %bitcast.10, bf16[216,256]{1,0:T(8,128)(2,1)S(1)} %bitcast.13), custom_call_target="tpu_custom_call" | custom-call | tf_op jit(solution)/shard_map/pallas_call | solution.py:546
  64.5 2.1 %copy.11 = bf16[2,8,2,16384]{3,2,1,0:T(2,128)(2,1)} copy(bf16[2,8,2,16384]{3,1,0,2:T(8,128)(2,1)S(1)} %bitcast.11) | data formatting | bytes 2097152
  66.5 0.1 copy.10
  66.7 0.8 %copy.12 = f32[27,8,16]{0,2,1:T(8,128)} copy(f32[27,8,16]{2,1,0:T(8,128)S(1)} %maximum_bitcast_fusion) | data formatting | bytes 27648
  (3 shorter events, 0.0 us)
Async XLA Ops:
  0.6 1.9 %copy-start = (bf16[2,16,1,4096]{3,1,2,0:T(8,128)(2,1)S(1)}, bf16[2,16,1,4096]{3,1,2,0:T(8,128)(2,1)}, u32[]{:S(2)}) copy-start(bf16[2,16,1,4096]{3,1,2,0:T(8,128)(2,1)} %param.4) | copy-start | bytes 786436
  0.6 1.9 %copy-start.1 = (bf16[27,8,256]{2,1,0:T(8,128)(2,1)S(1)}, bf16[27,8,256]{2,1,0:T(8,128)(2,1)}, u32[]{:S(2)}) copy-start(bf16[27,8,256]{2,1,0:T(8,128)(2,1)} %param.5) | copy-start | bytes 331780

commit v4 on v3

--- a/solution.py
+++ b/solution.py
@@ -17,6 +17,7 @@
 CHUNKS = 2 * PER_SAMPLE
 EARLY = tuple(range(9, 25))
 HALO_AT = 4
+AHEAD = 4
 CROSS = CHUNKS - 1
 LATE = (25, 26) + tuple(range(9))
 
@@ -25,9 +26,9 @@
     grad_hbm, planes_hbm, w_ref, out_ref, wg_ref,
     held, early, late, planes, groups, carry, share, share_in,
     odd, acc, pair_in, paired, near, relay, halo_relay,
-    local_sem, z_send, z_recv, y_send, y_recv, f_send, f_recv,
+    local_sem, z_send, z_recv, o_send, o_recv, y_send, y_recv, f_send, f_recv,
     halo_send, halo_recv, p_send, p_recv, q_send, q_recv, h_send, h_recv,
-    c_send, c_recv, r_send, r_recv, by_send, by_recv, bf_send, bf_recv, bz_send, bz_recv,
+    c_send, c_recv, r_send, r_recv, bf_send, bf_recv, bz_send, bz_recv,
 ):
     slab = lax.axis_index("slab")
     chan = lax.axis_index("chan")
@@ -104,12 +105,21 @@
 
     low, high = (y + 3) % 4, (y + 1) % 4
 
+    def y_own(k):
+        return [
+            remote(source(k), held.at[k, y, z], o_send.at[k, 0], o_recv.at[k, 0], y_up),
+            remote(source(k), held.at[k, y, z], o_send.at[k, 1], o_recv.at[k, 1], y_down),
+        ]
+
+    def y_piece(k, d):
+        piece = held.at[k, y, (z + 3 - d) % 4]
+        return [
+            remote(piece, piece, y_send.at[k, d, 0], y_recv.at[k, d, 0], y_up),
+            remote(piece, piece, y_send.at[k, d, 1], y_recv.at[k, d, 1], y_down),
+        ]
+
     def y_copies(k):
-        block = held.at[k, y]
-        return [
-            remote(block, block, y_send.at[k, 0], y_recv.at[k, 0], y_up),
-            remote(block, block, y_send.at[k, 1], y_recv.at[k, 1], y_down),
-        ]
+        return y_own(k) + y_piece(k, 0) + y_piece(k, 1) + y_piece(k, 2)
 
     def f_copies(k):
         from_low, from_high = held.at[k, low, pl.ds(0, 2)], held.at[k, high, pl.ds(2, 2)]
@@ -119,10 +129,7 @@
         ]
 
     def cross_y():
-        return [
-            remote(source(CROSS), held.at[CROSS, y, z], by_send.at[0], by_recv.at[0], y_up),
-            remote(source(CROSS), held.at[CROSS, y, z], by_send.at[1], by_recv.at[1], y_down),
-        ]
+        return y_own(CROSS)
 
     def cross_f():
         from_low = held.at[CROSS, low, z, :, pl.ds(0, CHUNK // 2)]
@@ -240,10 +247,10 @@
     def _():
         pl.semaphore_wait(barrier, len(peers))
 
-    for copy in cross_y():
+    for copy in z_copies(0) + cross_y():
         copy.start()
-    for k in range(4):
-        for copy in z_copies(k):
+    for k in range(CROSS):
+        for copy in y_own(k) + (z_copies(k) if 0 < k < AHEAD else []):
             copy.start()
 
     @pl.when((slab < 15) & (slab != 7))
@@ -290,11 +297,10 @@
                     ]
 
     def start_y(k):
-        local(k).wait()
-        for copy in z_copies(k):
+        for d, copy in enumerate(z_copies(k)):
             copy.wait_recv()
-        for copy in y_copies(k):
-            copy.start()
+            for onward in y_piece(k, d):
+                onward.start()
 
     def start_f(k):
         for copy in y_copies(k):
@@ -385,13 +391,14 @@
             odd[k % 2, phase] = value
 
     def receive(k):
+        local(k).wait()
         for copy in f_copies(k):
             copy.wait_recv()
 
     def step(k, _):
-        @pl.when(k + 4 < CROSS)
-        def _():
-            for copy in z_copies(k + 4):
+        @pl.when(k + AHEAD < CROSS)
+        def _():
+            for copy in z_copies(k + AHEAD):
                 copy.start()
 
         @pl.when(k + 2 < CROSS)
@@ -570,6 +577,7 @@
             sem((CHUNKS + 2,)),
             sem((CHUNKS, 3)), sem((CHUNKS, 3)),
             sem((CHUNKS, 2)), sem((CHUNKS, 2)),
+            sem((CHUNKS, 3, 2)), sem((CHUNKS, 3, 2)),
             sem((CHUNKS, 2)), sem((CHUNKS, 2)),
             sem((4,)), sem((4,)),
             sem((CHUNKS, 4)), sem((CHUNKS, 4)),
@@ -577,7 +585,6 @@
             sem, sem,
             sem, sem,
             sem((7,)), sem((7,)),
-            sem((2,)), sem((2,)),
             sem((2,)), sem((2,)),
             sem((2, 3)), sem((2, 3)),
         ],

time: 67.5 us -> 66.1 us (0.979); the launches traced: 67.4 us -> 65.3 us
  Pallas kernels: 61.9 us -> 59.8 us
    pallas_call x1, Pallas kernels: 61.9 us -> 59.8 us  [body(): pl.pallas_call(gather_kernel, out_shape=(jax.ShapeDtypeStruct((2, 2, 8, 4...]
where the time goes in v4:
time: 66.1 us; the launch traced here: 65.3 us
  Pallas kernels  59.8 us (90%)
  local copies, waits for them, and re-layouts  4.77 us (7%)
  between operations  0.69 us (1%)
    pallas_call x1, Pallas kernels, body(): pl.pallas_call(gather_kernel, out_shape=(jax.ShapeDtypeStruct((2, 2, 8, 4...  59.8 us
    unnamed x7, local copies, waits for them, and re-layouts  4.67 us

profile of v4, /device:TPU:1, one launch (start us, length us, event | category | flops | bytes accessed | tf_op | source)
XLA Modules:
  0.0 65.3 jit_solution(17754085810240904954)
XLA Ops:
  0.6 0.0 copy-start
  0.6 0.0 copy-start.1
  0.6 1.9 %copy.14 = bf16[2,8,2,16384]{3,1,0,2:T(8,128)(2,1)S(1)} copy(bf16[2,8,2,16384]{3,2,1,0:T(2,128)(2,1)} %param.3) | data formatting | bytes 2097152 | tf_op args[0]
  2.5 0.0 copy-done
  2.5 0.0 copy-done.1
  2.5 59.8 %shard_map.50 = (bf16[2,2,8,16384]{3,2,1,0:T(8,128)(2,1)S(1)}, f32[16,256]{1,0:T(8,128)S(1)}) custom-call(bf16[2,16,4096]{2,1,0:T(8,128)(2,1)S(1)} %bitcast.12, bf16[2,2,8,16384]{3,2,1,0:T(8,128)(2,1)S(1)} %bitcast.10, bf16[216,256]{1,0:T(8,128)(2,1)S(1)} %bitcast.13), custom_call_target="tpu_custom_call" | custom-call | tf_op jit(solution)/shard_map/pallas_call | solution.py:553
  62.4 2.1 %copy.11 = bf16[2,8,2,16384]{3,2,1,0:T(2,128)(2,1)} copy(bf16[2,8,2,16384]{3,1,0,2:T(8,128)(2,1)S(1)} %bitcast.11) | data formatting | bytes 2097152
  64.4 0.1 copy.10
  64.6 0.8 %copy.12 = f32[27,8,16]{0,2,1:T(8,128)} copy(f32[27,8,16]{2,1,0:T(8,128)S(1)} %maximum_bitcast_fusion) | data formatting | bytes 27648
  (3 shorter events, 0.0 us)
Async XLA Ops:
  0.6 1.9 %copy-start = (bf16[2,16,1,4096]{3,1,2,0:T(8,128)(2,1)S(1)}, bf16[2,16,1,4096]{3,1,2,0:T(8,128)(2,1)}, u32[]{:S(2)}) copy-start(bf16[2,16,1,4096]{3,1,2,0:T(8,128)(2,1)} %param.4) | copy-start | bytes 786436
  0.6 1.9 %copy-start.1 = (bf16[27,8,256]{2,1,0:T(8,128)(2,1)S(1)}, bf16[27,8,256]{2,1,0:T(8,128)(2,1)}, u32[]{:S(2)}) copy-start(bf16[27,8,256]{2,1,0:T(8,128)(2,1)} %param.5) | copy-start | bytes 331780

commit v5 on v4

--- a/solution.py
+++ b/solution.py
@@ -85,9 +85,18 @@
     def _():
         greet(at(7, chan))
 
+    def sample_of(k):
+        return ((k + 1) // PER_SAMPLE) % 2
+
+    def begin_of(k):
+        later = min(k // 3, 1) if isinstance(k, int) else lax.min(k // 3, 1)
+        return (PER_SAMPLE - 1 - k + 3 * later + k // CROSS) * CHUNK
+
+    def slot_of(k):
+        return k % 2 + k // CROSS
+
     def source(k):
-        begin = pl.multiple_of((PER_SAMPLE - 1 - k % PER_SAMPLE) * CHUNK, CHUNK)
-        return grad_hbm.at[k // PER_SAMPLE, :, pl.ds(begin, CHUNK)]
+        return grad_hbm.at[sample_of(k), :, pl.ds(pl.multiple_of(begin_of(k), CHUNK), CHUNK)]
 
     def local(k):
         return pltpu.make_async_copy(source(k), held.at[k, y, z], local_sem.at[k])
@@ -263,6 +272,7 @@
             halo_out(q).start()
 
     acc[...] = jnp.zeros_like(acc)
+    carry[...] = jnp.zeros_like(carry)
     load_even.wait()
     load_odd.wait()
 
@@ -292,7 +302,8 @@
                     rows.append(jnp.zeros_like(rows[0]))
                 both = jnp.concatenate(rows, axis=0).astype(jnp.bfloat16)
                 for j in range(PER_SAMPLE):
-                    store[sample * PER_SAMPLE + PER_SAMPLE - 1 - j, 16 * pair : 16 * pair + 16, :] = both[
+                    k = 6 - j if sample else (CROSS if j == 0 else 3 - j)
+                    store[k, 16 * pair : 16 * pair + 16, :] = both[
                         :, j * CHUNK : (j + 1) * CHUNK
                     ]
 
@@ -329,13 +340,13 @@
     def col_ahead(value):
         return jnp.where(last_col, 0.0, pltpu.roll(value, CHUNK - 1, 1))
 
-    def phases(depth_tap):
+    def phases(depth_tap, sample):
         def fetch(row_tap, col_tap):
             row = 8 * (9 * depth_tap + 3 * row_tap + col_tap)
             return groups[row : row + 8, :]
 
         def odd_row(col_tap):
-            at_carry = 3 * depth_tap + col_tap
+            at_carry = sample, 3 * depth_tap + col_tap
             moving = fetch(0, col_tap)
             moved = row_ahead(moving, carry[at_carry])
             carry[at_carry] = moving[:, :128]
@@ -350,8 +361,7 @@
         return found
 
     def lanes_of(k, phase):
-        begin = phase * CELLS + (PER_SAMPLE - 1 - k % PER_SAMPLE) * CHUNK
-        return pl.ds(pl.multiple_of(begin, CHUNK), CHUNK)
+        return pl.ds(pl.multiple_of(phase * CELLS + begin_of(k), CHUNK), CHUNK)
 
     def late_dot(k):
         term = lax.dot_general(
@@ -366,9 +376,9 @@
                 share_copy(k, q).wait_recv()
 
         for phase in range(4):
-            value = odd[k % 2, phase]
+            value = odd[slot_of(k), phase]
             inward = jnp.where(slab < 15, share_in[k, phase], 0.0)
-            out_ref[1, k // PER_SAMPLE, :, lanes_of(k, phase)] = (value + inward).astype(jnp.bfloat16)
+            out_ref[1, sample_of(k), :, lanes_of(k, phase)] = (value + inward).astype(jnp.bfloat16)
 
     def early_dot(k):
         term = lax.dot_general(
@@ -377,18 +387,14 @@
         acc[:, :, :, :, :128] += term.reshape(2, 4, 2, 16, 128)
 
     def input_part(k):
-        @pl.when(k % PER_SAMPLE == 0)
-        def _():
-            carry[...] = jnp.zeros_like(carry)
-
         groups[...] = jnp.dot(w_ref[...], held[k].reshape(256, CHUNK), preferred_element_type=jnp.float32)
-        for phase, value in enumerate(phases(0)):
+        for phase, value in enumerate(phases(0, sample_of(k))):
             share[k, phase] = value
         send_share(k)
-        for phase, value in enumerate(phases(1)):
-            out_ref[0, k // PER_SAMPLE, :, lanes_of(k, phase)] = value.astype(jnp.bfloat16)
-        for phase, value in enumerate(phases(2)):
-            odd[k % 2, phase] = value
+        for phase, value in enumerate(phases(1, sample_of(k))):
+            out_ref[0, sample_of(k), :, lanes_of(k, phase)] = value.astype(jnp.bfloat16)
+        for phase, value in enumerate(phases(2, sample_of(k))):
+            odd[slot_of(k), phase] = value
 
     def receive(k):
         local(k).wait()
@@ -478,6 +484,7 @@
     cross_recv(2)
     early_dot(CROSS)
     late_dot(CROSS)
+    input_part(CROSS)
     receive(tail)
     early_dot(tail)
     late_dot(tail)
@@ -488,12 +495,11 @@
     paired[...] = acc[:, :, core] + pair_in[...]
     for d in range(7):
         spread(d).start()
+    pass_share(CROSS)
     finish(tail - 1)
-    input_part(CROSS)
+    finish(CROSS)
     pass_share(tail)
     finish(tail)
-    pass_share(CROSS)
-    finish(CROSS)
     total = paired[half, column]
     for d in range(7):
         spread(d).wait_recv()
@@ -564,10 +570,10 @@
             pltpu.VMEM((CHUNKS, 96, CHUNK), bf16),
             pltpu.VMEM((3, 2, 8, 4 * CELLS), bf16),
             pltpu.VMEM((216, CHUNK), f32),
-            pltpu.VMEM((9, 8, 128), f32),
+            pltpu.VMEM((2, 9, 8, 128), f32),
             pltpu.VMEM((CHUNKS, 4, 8, CHUNK), f32),
             pltpu.VMEM((CHUNKS, 4, 8, CHUNK), f32),
-            pltpu.VMEM((2, 4, 8, CHUNK), f32),
+            pltpu.VMEM((3, 4, 8, CHUNK), f32),
             pltpu.VMEM((2, 4, 2, 16, 256), f32),
             pltpu.VMEM((2, 4, 16, 256), f32),
             pltpu.VMEM((2, 4, 16, 256), f32),

time: 66.1 us -> 64.5 us (0.976); the launches traced: 65.3 us -> 64.4 us
  Pallas kernels: 59.8 us -> 58.9 us
    pallas_call x1, Pallas kernels: 59.8 us -> 58.9 us  [body(): pl.pallas_call(gather_kernel, out_shape=(jax.ShapeDtypeStruct((2, 2, 8, 4...]
where the time goes in v5:
time: 64.5 us; the launch traced here: 64.4 us
  Pallas kernels  58.9 us (91%)
  local copies, waits for them, and re-layouts  4.77 us (7%)
  between operations  0.69 us (1%)
    pallas_call x1, Pallas kernels, body(): pl.pallas_call(gather_kernel, out_shape=(jax.ShapeDtypeStruct((2, 2, 8, 4...  58.9 us
    unnamed x7, local copies, waits for them, and re-layouts  4.67 us

profile of v5, /device:TPU:1, one launch (start us, length us, event | category | flops | bytes accessed | tf_op | source)
XLA Modules:
  0.0 64.4 jit_solution(2351225698976636279)
XLA Ops:
  0.6 0.0 copy-start
  0.6 0.0 copy-start.1
  0.6 1.9 %copy.14 = bf16[2,8,2,16384]{3,1,0,2:T(8,128)(2,1)S(1)} copy(bf16[2,8,2,16384]{3,2,1,0:T(2,128)(2,1)} %param.3) | data formatting | bytes 2097152 | tf_op args[0]
  2.5 0.0 copy-done
  2.5 0.0 copy-done.1
  2.5 58.9 %shard_map.50 = (bf16[2,2,8,16384]{3,2,1,0:T(8,128)(2,1)S(1)}, f32[16,256]{1,0:T(8,128)S(1)}) custom-call(bf16[2,16,4096]{2,1,0:T(8,128)(2,1)S(1)} %bitcast.12, bf16[2,2,8,16384]{3,2,1,0:T(8,128)(2,1)S(1)} %bitcast.10, bf16[216,256]{1,0:T(8,128)(2,1)S(1)} %bitcast.13), custom_call_target="tpu_custom_call" | custom-call | tf_op jit(solution)/shard_map/pallas_call | solution.py:559
  61.5 2.1 %copy.11 = bf16[2,8,2,16384]{3,2,1,0:T(2,128)(2,1)} copy(bf16[2,8,2,16384]{3,1,0,2:T(8,128)(2,1)S(1)} %bitcast.11) | data formatting | bytes 2097152
  63.5 0.1 copy.10
  63.7 0.8 %copy.12 = f32[27,8,16]{0,2,1:T(8,128)} copy(f32[27,8,16]{2,1,0:T(8,128)S(1)} %maximum_bitcast_fusion) | data formatting | bytes 27648
  (3 shorter events, 0.0 us)
Async XLA Ops:
  0.6 1.9 %copy-start = (bf16[2,16,1,4096]{3,1,2,0:T(8,128)(2,1)S(1)}, bf16[2,16,1,4096]{3,1,2,0:T(8,128)(2,1)}, u32[]{:S(2)}) copy-start(bf16[2,16,1,4096]{3,1,2,0:T(8,128)(2,1)} %param.4) | copy-start | bytes 786436
  0.6 1.9 %copy-start.1 = (bf16[27,8,256]{2,1,0:T(8,128)(2,1)S(1)}, bf16[27,8,256]{2,1,0:T(8,128)(2,1)}, u32[]{:S(2)}) copy-start(bf16[27,8,256]{2,1,0:T(8,128)(2,1)} %param.5) | copy-start | bytes 331780

commit v6 on v5

--- a/solution.py
+++ b/solution.py
@@ -25,7 +25,7 @@
 def gather_kernel(
     grad_hbm, planes_hbm, w_ref, out_ref, wg_ref,
     held, early, late, planes, groups, carry, share, share_in,
-    odd, acc, pair_in, paired, near, relay, halo_relay,
+    even, odd, mixed, acc, pair_in, paired, near, relay, halo_relay,
     local_sem, z_send, z_recv, o_send, o_recv, y_send, y_recv, f_send, f_recv,
     halo_send, halo_recv, p_send, p_recv, q_send, q_recv, h_send, h_recv,
     c_send, c_recv, r_send, r_recv, bf_send, bf_recv, bz_send, bz_recv,
@@ -378,7 +378,15 @@
         for phase in range(4):
             value = odd[slot_of(k), phase]
             inward = jnp.where(slab < 15, share_in[k, phase], 0.0)
-            out_ref[1, sample_of(k), :, lanes_of(k, phase)] = (value + inward).astype(jnp.bfloat16)
+            value = value + inward
+            same = even[slot_of(k), phase]
+            blocks = []
+            for b in range(CHUNK // 128):
+                cut = slice(b * 128, b * 128 + 128)
+                mixed[phase, b, pl.ds(0, 8, 2), :] = same[:, cut]
+                mixed[phase, b, pl.ds(1, 8, 2), :] = value[:, cut]
+                blocks.append(mixed[phase, b])
+            out_ref[sample_of(k), :, lanes_of(k, phase)] = jnp.concatenate(blocks, axis=1).astype(jnp.bfloat16)
 
     def early_dot(k):
         term = lax.dot_general(
@@ -392,7 +400,7 @@
             share[k, phase] = value
         send_share(k)
         for phase, value in enumerate(phases(1, sample_of(k))):
-            out_ref[0, sample_of(k), :, lanes_of(k, phase)] = value.astype(jnp.bfloat16)
+            even[slot_of(k), phase] = value
         for phase, value in enumerate(phases(2, sample_of(k))):
             odd[slot_of(k), phase] = value
 
@@ -559,7 +567,7 @@
     out, wg = pl.pallas_call(
         gather_kernel,
         out_shape=(
-            jax.ShapeDtypeStruct((2, 2, 8, 4 * CELLS), bf16),
+            jax.ShapeDtypeStruct((2, 16, 4 * CELLS), bf16),
             jax.ShapeDtypeStruct((16, 256), f32),
         ),
         in_specs=[any_space, any_space, vmem],
@@ -574,6 +582,8 @@
             pltpu.VMEM((CHUNKS, 4, 8, CHUNK), f32),
             pltpu.VMEM((CHUNKS, 4, 8, CHUNK), f32),
             pltpu.VMEM((3, 4, 8, CHUNK), f32),
+            pltpu.VMEM((3, 4, 8, CHUNK), f32),
+            pltpu.VMEM((4, CHUNK // 128, 16, 128), f32),
             pltpu.VMEM((2, 4, 2, 16, 256), f32),
             pltpu.VMEM((2, 4, 16, 256), f32),
             pltpu.VMEM((2, 4, 16, 256), f32),
@@ -598,7 +608,7 @@
             collective_id=0, has_side_effects=True, vmem_limit_bytes=48 * 1024 * 1024
         ),
     )(grad, planes, w)
-    input_grad = out.transpose(1, 2, 0, 3)
+    input_grad = out.reshape(2, 8, 2, 4 * CELLS)
     taps = wg[:, :216].reshape(16, 27, 8)
     taps = jnp.concatenate([taps[:, 18:], taps[:, :18]], axis=1)
     return input_grad, taps.transpose(1, 2, 0)

time: 64.5 us -> 64 us (level)
    unnamed x7 -> x6, local copies, waits for them, and re-layouts: 4.67 us -> 2.61 us
    reshape x0 -> x1, local copies, waits for them, and re-layouts: none -> 1.5 us  [body(): input_grad = out.reshape(2, 8, 2, 4 * CELLS)]
where the time goes in v6:
time: 64 us; the launch traced here: 63.9 us
  Pallas kernels  59 us (92%)
  local copies, waits for them, and re-layouts  4.22 us (7%)
  between operations  0.69 us (1%)
    pallas_call x1, Pallas kernels, body(): pl.pallas_call(gather_kernel, out_shape=(jax.ShapeDtypeStruct((2, 16, 4 *...  59 us
    unnamed x6, local copies, waits for them, and re-layouts  2.61 us
    reshape x1, local copies, waits for them, and re-layouts, body(): input_grad = out.reshape(2, 8, 2, 4 * CELLS)  1.5 us

profile of v6, /device:TPU:1, one launch (start us, length us, event | category | flops | bytes accessed | tf_op | source)
XLA Modules:
  0.0 63.9 jit_solution(9366818320273718227)
XLA Ops:
  0.6 0.0 copy-start
  0.6 0.0 copy-start.1
  0.6 1.9 %copy.12 = bf16[2,8,2,16384]{3,1,0,2:T(8,128)(2,1)S(1)} copy(bf16[2,8,2,16384]{3,2,1,0:T(2,128)(2,1)} %param.3) | data formatting | bytes 2097152 | tf_op args[0]
  2.5 0.0 copy-done
  2.5 0.0 copy-done.1
  2.5 59.0 %shard_map.50 = (bf16[2,16,16384]{2,1,0:T(8,128)(2,1)S(1)}, f32[16,256]{1,0:T(8,128)S(1)}) custom-call(bf16[2,16,4096]{2,1,0:T(8,128)(2,1)S(1)} %bitcast.10, bf16[2,2,8,16384]{3,2,1,0:T(8,128)(2,1)S(1)} %bitcast.9, bf16[216,256]{1,0:T(8,128)(2,1)S(1)} %bitcast.11), custom_call_target="tpu_custom_call" | custom-call | tf_op jit(solution)/shard_map/pallas_call | solution.py:567
  61.5 1.5 %reshape.18 = bf16[2,8,2,16384]{3,2,1,0:T(2,128)(2,1)} reshape(bf16[2,16,16384]{2,1,0:T(8,128)(2,1)S(1)} %get-tuple-element.4) | data formatting | bytes 2097152 | tf_op jit(solution)/shard_map/reshape | solution.py:611
  63.0 0.1 copy.9
  63.1 0.8 %copy.10 = f32[27,8,16]{0,2,1:T(8,128)} copy(f32[27,8,16]{2,1,0:T(8,128)S(1)} %maximum_bitcast_fusion) | data formatting | bytes 27648
  (3 shorter events, 0.0 us)
Async XLA Ops:
  0.6 1.9 %copy-start = (bf16[2,16,1,4096]{3,1,2,0:T(8,128)(2,1)S(1)}, bf16[2,16,1,4096]{3,1,2,0:T(8,128)(2,1)}, u32[]{:S(2)}) copy-start(bf16[2,16,1,4096]{3,1,2,0:T(8,128)(2,1)} %param.4) | copy-start | bytes 786436
  0.6 1.9 %copy-start.1 = (bf16[27,8,256]{2,1,0:T(8,128)(2,1)S(1)}, bf16[27,8,256]{2,1,0:T(8,128)(2,1)}, u32[]{:S(2)}) copy-start(bf16[27,8,256]{2,1,0:T(8,128)(2,1)} %param.5) | copy-start | bytes 331780

commit v7 on v6

--- a/solution.py
+++ b/solution.py
@@ -93,7 +93,7 @@
         return (PER_SAMPLE - 1 - k + 3 * later + k // CROSS) * CHUNK
 
     def slot_of(k):
-        return k % 2 + k // CROSS
+        return k % 3 + 2 * (k // CROSS)
 
     def source(k):
         return grad_hbm.at[sample_of(k), :, pl.ds(pl.multiple_of(begin_of(k), CHUNK), CHUNK)]
@@ -474,7 +474,10 @@
         @pl.when(k >= 1)
         def _():
             pass_share(k - 1)
-            finish(k - 1)
+
+        @pl.when(k >= 2)
+        def _():
+            finish(k - 2)
 
         return 0
 
@@ -504,6 +507,7 @@
     for d in range(7):
         spread(d).start()
     pass_share(CROSS)
+    finish(tail - 2)
     finish(tail - 1)
     finish(CROSS)
     pass_share(tail)
@@ -581,8 +585,8 @@
             pltpu.VMEM((2, 9, 8, 128), f32),
             pltpu.VMEM((CHUNKS, 4, 8, CHUNK), f32),
             pltpu.VMEM((CHUNKS, 4, 8, CHUNK), f32),
-            pltpu.VMEM((3, 4, 8, CHUNK), f32),
-            pltpu.VMEM((3, 4, 8, CHUNK), f32),
+            pltpu.VMEM((4, 4, 8, CHUNK), f32),
+            pltpu.VMEM((4, 4, 8, CHUNK), f32),
             pltpu.VMEM((4, CHUNK // 128, 16, 128), f32),
             pltpu.VMEM((2, 4, 2, 16, 256), f32),
             pltpu.VMEM((2, 4, 16, 256), f32),

time: 64 us -> 63.9 us (level)
  no operation moved by 1% of the time
where the time goes in v7:
time: 63.9 us; the launch traced here: 63.6 us
  Pallas kernels  58.7 us (92%)
  local copies, waits for them, and re-layouts  4.22 us (7%)
  between operations  0.69 us (1%)
    pallas_call x1, Pallas kernels, body(): pl.pallas_call(gather_kernel, out_shape=(jax.ShapeDtypeStruct((2, 16, 4 *...  58.7 us
    unnamed x6, local copies, waits for them, and re-layouts  2.61 us
    reshape x1, local copies, waits for them, and re-layouts, body(): input_grad = out.reshape(2, 8, 2, 4 * CELLS)  1.5 us

profile of v7, /device:TPU:1, one launch (start us, length us, event | category | flops | bytes accessed | tf_op | source)
XLA Modules:
  0.0 63.6 jit_solution(10125328101167534916)
XLA Ops:
  0.6 0.0 copy-start
  0.6 0.0 copy-start.1
  0.6 1.9 %copy.12 = bf16[2,8,2,16384]{3,1,0,2:T(8,128)(2,1)S(1)} copy(bf16[2,8,2,16384]{3,2,1,0:T(2,128)(2,1)} %param.3) | data formatting | bytes 2097152 | tf_op args[0]
  2.5 0.0 copy-done
  2.5 0.0 copy-done.1
  2.5 58.7 %shard_map.50 = (bf16[2,16,16384]{2,1,0:T(8,128)(2,1)S(1)}, f32[16,256]{1,0:T(8,128)S(1)}) custom-call(bf16[2,16,4096]{2,1,0:T(8,128)(2,1)S(1)} %bitcast.10, bf16[2,2,8,16384]{3,2,1,0:T(8,128)(2,1)S(1)} %bitcast.9, bf16[216,256]{1,0:T(8,128)(2,1)S(1)} %bitcast.11), custom_call_target="tpu_custom_call" | custom-call | tf_op jit(solution)/shard_map/pallas_call | solution.py:571
  61.3 1.5 %reshape.18 = bf16[2,8,2,16384]{3,2,1,0:T(2,128)(2,1)} reshape(bf16[2,16,16384]{2,1,0:T(8,128)(2,1)S(1)} %get-tuple-element.4) | data formatting | bytes 2097152 | tf_op jit(solution)/shard_map/reshape | solution.py:615
  62.7 0.1 copy.9
  62.9 0.8 %copy.10 = f32[27,8,16]{0,2,1:T(8,128)} copy(f32[27,8,16]{2,1,0:T(8,128)S(1)} %maximum_bitcast_fusion) | data formatting | bytes 27648
  (3 shorter events, 0.0 us)
Async XLA Ops:
  0.6 1.9 %copy-start = (bf16[2,16,1,4096]{3,1,2,0:T(8,128)(2,1)S(1)}, bf16[2,16,1,4096]{3,1,2,0:T(8,128)(2,1)}, u32[]{:S(2)}) copy-start(bf16[2,16,1,4096]{3,1,2,0:T(8,128)(2,1)} %param.4) | copy-start | bytes 786436
  0.6 1.9 %copy-start.1 = (bf16[27,8,256]{2,1,0:T(8,128)(2,1)S(1)}, bf16[27,8,256]{2,1,0:T(8,128)(2,1)}, u32[]{:S(2)}) copy-start(bf16[27,8,256]{2,1,0:T(8,128)(2,1)} %param.5) | copy-start | bytes 331780
